TPU v7x, 32 devices: a whole 2x2x4 slice. The times are simulated.
32 devices in a mesh: ctx: 8 (over z, x), head: 4 (over y, core).
Axes of the slice: x: 2, y: 2, z: 4, core: 2. Of those that a mesh axis runs over, the one named last changes fastest.
Arguments:
- query: bfloat16 [8, 2, 128, 8192], P('ctx', None, 'head'), may hold values from -200 to 200
- keyval: bfloat16 [8, 2, 2, 128, 1024], P('ctx', None, None, 'head'), may hold values from -6 to 6
- doc_blocks: int32 [4], replicated, may hold values from 1 to 12, 16 in all
Outputs:
- attended: bfloat16 [8, 2, 128, 8192], P('ctx', None, 'head')
Inputs may be any that keep to these rules, and one draw needn't show every extreme that they name: `doc_blocks`: documents fill the sequence in order; the longest has exactly 12 blocks.
All inputs are finite; a program needn't handle non-finite values.
Results may differ from a plain program's by a relative error of at most 0.0038.
Values may be sent and summed in bfloat16 or wider, within the bound.
A program may use at most 64 MiB of HBM per device.

v0:
```python
import jax
import jax.numpy as jnp
from jax import lax
from jax.sharding import PartitionSpec as P

QUERY_HEADS = 64
KEY_VALUE_HEADS = 8
HEAD_WIDTH = 128
BLK = 128


def doc_index(positions, doc_ends):
    return jnp.sum((positions[:, None] >= doc_ends[None, :]).astype(jnp.int32), axis=1)


def local(query, keyval, doc_blocks):
    ctx_count = lax.axis_size("ctx")
    ctx_index = lax.axis_index("ctx")
    span_len = query.shape[2] * lax.axis_size("head")
    width_kv = keyval.shape[4]
    stacked = keyval.reshape(1, 4, keyval.shape[3], width_kv)
    query_heads, kv_heads = (
        lax.all_to_all(query, "head", split_axis=3, concat_axis=2, tiled=True),
        lax.all_to_all(stacked, "head", split_axis=3, concat_axis=2, tiled=True),
    )
    kv_local = kv_heads.shape[3] // HEAD_WIDTH
    heads_per_group = QUERY_HEADS // KEY_VALUE_HEADS
    kv_mine = kv_heads.reshape(1, 2, 2, span_len, kv_local * HEAD_WIDTH)
    row_count = 2 * span_len
    query_rows = query_heads.reshape(row_count, kv_local, heads_per_group, HEAD_WIDTH)
    offsets = jnp.arange(span_len, dtype=jnp.int32)
    query_pos = jnp.concatenate(
        [ctx_index * span_len + offsets, (2 * ctx_count - 1 - ctx_index) * span_len + offsets]
    )
    doc_ends = jnp.cumsum(doc_blocks) * BLK
    query_doc = doc_index(query_pos, doc_ends)
    scale_factor = HEAD_WIDTH ** (-0.5)
    initial = (
        jnp.full((kv_local, heads_per_group, row_count), -1e30, jnp.float32),
        jnp.zeros((kv_local, heads_per_group, row_count), jnp.float32),
        jnp.zeros((row_count, kv_local, heads_per_group, HEAD_WIDTH), jnp.float32),
    )
    gathered = lax.all_gather(kv_mine, "ctx", axis=0, tiled=True)
    running = initial
    count = gathered.shape[0]
    group_size = 4
    group_count = count // group_size
    grouped = gathered.reshape(group_count, group_size, 2, 2, span_len, kv_local * HEAD_WIDTH)
    firsts = jnp.arange(group_count, dtype=jnp.int32) * group_size

    def advance(state, payload):
        block_kv, lead_span = payload
        span_ids = lead_span + jnp.arange(group_size, dtype=jnp.int32)
        lower_pos = span_ids[:, None] * span_len + offsets[None, :]
        upper_pos = (2 * ctx_count - 1 - span_ids)[:, None] * span_len + offsets[None, :]
        key_pos = jnp.stack([lower_pos, upper_pos], axis=1).reshape(-1)
        key_row_block = block_kv[:, 0].reshape(-1, kv_local, HEAD_WIDTH)
        value_rows = block_kv[:, 1].reshape(-1, kv_local, HEAD_WIDTH)
        visible = (query_doc[:, None] == doc_index(key_pos, doc_ends)[None, :]) & (
            key_pos[None, :] <= query_pos[:, None]
        )
        row_max, totals, acc_sum = state
        scores = (
            jnp.einsum(
                "rgjd,kgd->gjrk", query_rows, key_row_block, preferred_element_type=jnp.float32
            )
            * scale_factor
        )
        scores = jnp.where(visible[None, None], scores, -1e30)
        new_max = jnp.maximum(row_max, jnp.max(scores, axis=-1))
        probs = jnp.where(visible[None, None], jnp.exp(scores - new_max[..., None]), 0.0)
        rescale = jnp.exp(row_max - new_max)
        totals = totals * rescale + jnp.sum(probs, axis=-1)
        added = jnp.einsum(
            "gjrk,kgd->rgjd",
            probs.astype(jnp.bfloat16),
            value_rows,
            preferred_element_type=jnp.float32,
        )
        acc_sum = acc_sum * jnp.moveaxis(rescale, 2, 0)[..., None] + added
        state = (new_max, totals, acc_sum)
        return (state, None)

    running, _ = lax.scan(advance, running, (grouped, firsts))
    row_max, totals, acc_sum = running
    result = (acc_sum / jnp.moveaxis(totals, 2, 0)[..., None]).astype(jnp.bfloat16)
    result = result.reshape(1, 2, span_len, kv_local * heads_per_group * HEAD_WIDTH)
    return lax.all_to_all(result, "head", split_axis=2, concat_axis=3, tiled=True)


def solution(mesh):
    placed = (P("ctx", None, "head", None), P("ctx", None, None, "head", None), P())
    return jax.shard_map(
        local, mesh=mesh, in_specs=placed, out_specs=P("ctx", None, "head", None), check_vma=False
    )
```

profile of v0, /device:TPU:0, one launch (start us, length us, event | category | flops | bytes accessed | tf_op | source)
XLA Modules:
  0.0 154.3 jit_solution(14284918072613798459)
XLA Ops:
  6.5 2.2 %copy.50 = bf16[1,2,2,32,1024]{3,2,1,4,0:T(2,128)(2,1)S(1)} copy(bf16[1,2,2,32,1024]{4,3,2,1,0:T(8,128)(2,1)} %param.6) | data formatting | bytes 524288 | tf_op args[1]
  8.8 1.0 reshape.201
  9.7 10.1 %all_to_all.48 = bf16[4,2,16384]{2,1,0:T(2,128)(2,1)S(1)} all-to-all(bf16[4,2,16384]{2,1,0:T(2,128)(2,1)S(1)} %reshape.201), channel_id=1, replica_groups=mesh['ctx'=8,'head'=4] {'head'}, dimensions={0} | all-to-all | bytes 524288 | tf_op jit(solution)/shard_map/all_to_all | solution.py:24
  19.8 0.5 reshape.202
  20.3 0.7 copy.64
  21.0 0.7 copy.52
  21.8 9.2 %copy.53 = bf16[1,2,32,8192]{2,1,0,3:T(2,128)(2,1)} copy(bf16[1,2,32,8192]{3,2,1,0:T(8,128)(2,1)} %param.5) | data formatting | bytes 2097152 | tf_op args[0]
  30.9 6.4 %reshape.203 = bf16[4,2,65536]{2,1,0:T(2,128)(2,1)} reshape(bf16[8192,1,2,32]{3,2,1,0:T(2,128)(2,1)} %bitcast.85) | data formatting | bytes 2097152
  37.3 3.5 %all-to-all-start.1 = ((bf16[4,2,65536]{2,1,0:T(2,128)(2,1)}), bf16[4,2,65536]{2,1,0:T(2,128)(2,1)S(1)}, u32[]{:S(2)}, u32[]{:S(2)}) async-start(bf16[4,2,65536]{2,1,0:T(2,128)(2,1)} %reshape.203), calls=%async_computation.1 | async-start | bytes 2097152 | tf_op jit(solution)/shard_map/all_to_all | solution.py:23
  41.2 14.1 %all-to-all-done.1 = bf16[4,2,65536]{2,1,0:T(2,128)(2,1)S(1)} async-done(((bf16[4,2,65536]{2,1,0:T(2,128)(2,1)}), bf16[4,2,65536]{2,1,0:T(2,128)(2,1)S(1)}, u32[]{:S(2)}, u32[]{:S(2)}) %all-to-all-start.1) | async-done | bytes 1048608 | tf_op jit(solution)/shard_map/all_to_all | solution.py:23
  55.3 3.5 %reshape.204 = bf16[8192,1,2,32]{3,2,1,0:T(2,128)(2,1)} reshape(bf16[4,2,65536]{2,1,0:T(2,128)(2,1)S(1)} %all-to-all-done.1) | data formatting | bytes 2097152
  58.8 9.0 %copy.54 = bf16[1,2,32,4,2048]{4,2,3,1,0:T(8,128)(2,1)S(1)} copy(bf16[1,2,32,4,2048]{2,1,4,3,0:T(2,128)(2,1)} %bitcast.84) | data formatting | bytes 2097152 | tf_op jit(solution)/shard_map/all_to_all | solution.py:23
  68.3 3.1 %all-gather.2.cloned.1.call-done = bf16[8,2,2,128,256]{4,3,2,1,0:T(8,128)(2,1)} async-done(((bf16[1,2,2,128,256]{4,3,2,1,0:T(8,128)(2,1)}), bf16[8,2,2,128,256]{4,3,2,1,0:T(8,128)(2,1)}) %all-gather.2.cloned.1.call-update) | async-done | bytes 2097168 | tf_op jit(solution)/shard_map/all_gather | solution.py:43
  71.3 52.6 %while.16 = (s32[]{:T(128)}, f32[2,8,256]{2,1,0:T(8,128)S(1)}, f32[2,8,256]{2,1,0:T(8,128)S(1)}, f32[256,2,8,128]{0,3,2,1:T(8,128)}, s32[256]{0:T(256)S(1)}, /*i...) while((s32[]{:T(128)}, f32[2,8,256]{2,1,0:T(8,128)S(1)}, ...), condition=%wide.region_6.7_spmd.clone.clone, body=%wide.region_2.6_spmd.clone.clone.sunk | while | flops 2204406784 | bytes 131365624 | solution.py:84
  71.3 0.6 dynamic_slice.17
  71.9 0.6 subtract_multiply_fusion.2
  73.2 1.3 copy_bitcast_fusion.2
  74.7 7.2 %fusion.33 = (f32[2,8,256]{2,1,0:T(8,128)S(1)}, f32[2,1024,256,8]{2,1,3,0:T(8,128)}) fusion(pred[256,1024]{0,1:T(8,128)(4,1)S(1)} %compare_and_fusion.2, bf16[256,2,8,128]{3,0,2,1:T(8,128)(2,1)S(1)} %get-tuple-element.319, bf16[1024,2,128,1]{2,1,0,3:T(2,128)(2,1)S(1)} %bitcast.83), kind=kOutput, calls=%fused_computation.3.clone.1 | convolution fusion | flops 1086320640 | bytes 18628608 | tf_op jit(solution)/shard_map/while/body/eval_jaxpr/rgjd,kgd->gjrk/dot_general | solution.py:64
  82.0 9.7 %bitcast_add_fusion.2 = f32[256,2,8,128]{0,3,2,1:T(8,128)} fusion(f32[256,2,8,128]{0,3,2,1:T(8,128)} %get-tuple-element.301, f32[2,1024,256,8]{2,1,3,0:T(8,128)} %get-tuple-element.283, f32[2,8,256]{2,1,0:T(8,128)S(1)} %get-tuple-element.311, pred[256,1024]{0,1:T(8,128)(4,1)S(1)} %compare_and_fusion.2, f32[256,2,8]{0,2,1:T(8,128)S(1)} %get-tuple-element.284, ...), kind=kOutput, calls=%fused_computation.8.clone.1 | convolution fusion | flops 1096286208 | bytes 21790720 | tf_op jit(solution)/shard_map/while/body/eval_jaxpr/gjrk,kgd->rgjd/dot_general | solution.py:74
  91.7 1.6 %copy-done = f32[2,1024,256,8]{2,1,3,0:T(8,128)S(1)} copy-done((f32[2,1024,256,8]{2,1,3,0:T(8,128)S(1)}, f32[2,1024,256,8]{2,1,3,0:T(8,128)}, u32[]{:S(2)}) %copy-start) | copy-done | bytes 16777240 | tf_op jit(solution)/shard_map/while
  93.3 4.0 %fusion.35 = f32[2,8,256]{2,1,0:T(8,128)S(1)} fusion(f32[2,1024,256,8]{2,1,3,0:T(8,128)S(1)} %copy-done, f32[2,8,256]{2,1,0:T(8,128)S(1)} %get-tuple-element.311, pred[256,1024]{0,1:T(8,128)(4,1)S(1)} %compare_and_fusion.2), kind=kLoop, calls=%fused_computation.5.clone.1 | loop fusion | flops 20967424 | bytes 17072128 | tf_op jit(solution)/shard_map/while/body/eval_jaxpr/reduce_sum | solution.py:73
  97.4 0.6 dynamic_slice.17
  97.9 0.6 subtract_multiply_fusion.2
  99.2 1.3 copy_bitcast_fusion.2
  100.7 7.2 %fusion.33 = (f32[2,8,256]{2,1,0:T(8,128)S(1)}, f32[2,1024,256,8]{2,1,3,0:T(8,128)}) fusion(pred[256,1024]{0,1:T(8,128)(4,1)S(1)} %compare_and_fusion.2, bf16[256,2,8,128]{3,0,2,1:T(8,128)(2,1)S(1)} %get-tuple-element.319, bf16[1024,2,128,1]{2,1,0,3:T(2,128)(2,1)S(1)} %bitcast.83), kind=kOutput, calls=%fused_computation.3.clone.1 | convolution fusion | flops 1086320640 | bytes 18628608 | tf_op jit(solution)/shard_map/while/body/eval_jaxpr/rgjd,kgd->gjrk/dot_general | solution.py:64
  108.1 10.3 %bitcast_add_fusion.2 = f32[256,2,8,128]{0,3,2,1:T(8,128)} fusion(f32[256,2,8,128]{0,3,2,1:T(8,128)} %get-tuple-element.301, f32[2,1024,256,8]{2,1,3,0:T(8,128)} %get-tuple-element.283, f32[2,8,256]{2,1,0:T(8,128)S(1)} %get-tuple-element.311, pred[256,1024]{0,1:T(8,128)(4,1)S(1)} %compare_and_fusion.2, f32[256,2,8]{0,2,1:T(8,128)S(1)} %get-tuple-element.284, ...), kind=kOutput, calls=%fused_computation.8.clone.1 | convolution fusion | flops 1096286208 | bytes 21790720 | tf_op jit(solution)/shard_map/while/body/eval_jaxpr/gjrk,kgd->rgjd/dot_general | solution.py:74
  118.3 1.6 %copy-done = f32[2,1024,256,8]{2,1,3,0:T(8,128)S(1)} copy-done((f32[2,1024,256,8]{2,1,3,0:T(8,128)S(1)}, f32[2,1024,256,8]{2,1,3,0:T(8,128)}, u32[]{:S(2)}) %copy-start) | copy-done | bytes 16777240 | tf_op jit(solution)/shard_map/while
  119.9 4.0 %fusion.35 = f32[2,8,256]{2,1,0:T(8,128)S(1)} fusion(f32[2,1024,256,8]{2,1,3,0:T(8,128)S(1)} %copy-done, f32[2,8,256]{2,1,0:T(8,128)S(1)} %get-tuple-element.311, pred[256,1024]{0,1:T(8,128)(4,1)S(1)} %compare_and_fusion.2), kind=kLoop, calls=%fused_computation.5.clone.1 | loop fusion | flops 20967424 | bytes 17072128 | tf_op jit(solution)/shard_map/while/body/eval_jaxpr/reduce_sum | solution.py:73
  124.0 1.8 %divide_convert_fusion = bf16[256,2,8,128]{0,3,2,1:T(8,128)(2,1)S(1)} fusion(f32[256,2,8,128]{0,3,2,1:T(8,128)} %get-tuple-element.66, f32[256,2,8]{0,2,1:T(8,128)S(1)} %bitcast.97), kind=kLoop, calls=%fused_computation.31 | loop fusion | flops 1048576 | bytes 3162112 | tf_op jit(solution)/shard_map/convert_element_type | solution.py:86
  126.1 3.1 %copy.58 = bf16[1,2,128,2048]{3,1,0,2:T(2,128)(2,1)S(1)} copy(bf16[1,2,128,2048]{2,1,3,0:T(2,128)(2,1)S(1)} %reshape.199) | data formatting | bytes 2097152 | tf_op jit(solution)/shard_map/reshape | solution.py:87
  129.1 17.0 %all_to_all.49 = bf16[1,2,128,2048]{3,1,0,2:T(2,128)(2,1)S(1)} all-to-all(bf16[1,2,128,2048]{3,1,0,2:T(2,128)(2,1)S(1)} %copy.58), channel_id=1, replica_groups=mesh['ctx'=8,'head'=4] {'head'}, dimensions={2} | all-to-all | bytes 2097152 | tf_op jit(solution)/shard_map/all_to_all | solution.py:88
  146.5 1.0 copy.73
  (41 shorter events, 3.3 us)
Async XLA Ops:
  6.5 34.4 %copy-start.1 = (s32[4]{0:T(128)S(1)}, s32[4]{0:T(128)}, u32[]{:S(2)}) copy-start(s32[4]{0:T(128)} %param.7) | copy-start | bytes 52
  6.5 64.8 %all-gather.2.cloned.1.call-start = ((), (), s32[]{:S(2)}) async-start(), calls=%async_computation.3 | async-start | bytes 2359296 | tf_op jit(solution)/shard_map/all_gather | solution.py:43
  37.3 17.9 %all-to-all-start.1 = ((bf16[4,2,65536]{2,1,0:T(2,128)(2,1)}), bf16[4,2,65536]{2,1,0:T(2,128)(2,1)S(1)}, u32[]{:S(2)}, u32[]{:S(2)}) async-start(bf16[4,2,65536]{2,1,0:T(2,128)(2,1)} %reshape.203), calls=%async_computation.1 | async-start | bytes 2097152 | tf_op jit(solution)/shard_map/all_to_all | solution.py:23
  82.0 11.3 %copy-start = (f32[2,1024,256,8]{2,1,3,0:T(8,128)S(1)}, f32[2,1024,256,8]{2,1,3,0:T(8,128)}, u32[]{:S(2)}) copy-start(f32[2,1024,256,8]{2,1,3,0:T(8,128)} %get-tuple-element.283) | copy-start | bytes 50331652 | tf_op jit(solution)/shard_map/while
  108.0 11.9 %copy-start = (f32[2,1024,256,8]{2,1,3,0:T(8,128)S(1)}, f32[2,1024,256,8]{2,1,3,0:T(8,128)}, u32[]{:S(2)}) copy-start(f32[2,1024,256,8]{2,1,3,0:T(8,128)} %get-tuple-element.283) | copy-start | bytes 50331652 | tf_op jit(solution)/shard_map/while
Sparse Core Ops, SparseCore 0:
  21.9 49.4 all-gather.1
where the time goes:
time: 156 us; the launch traced here: 154 us
  local copies, waits for them, and re-layouts  46 us (29%)
  matrix products  34.3 us (22%)
  blocking collectives  27 us (17%)
  waiting for transfers between devices  17.2 us (11%)
  between operations  13.5 us (9%)
  other arithmetic  12.5 us (8%)
  starting transfers between devices  3.52 us (2%)
    unnamed x10, local copies, waits for them, and re-layouts  23.3 us
    dot_general x2, matrix products, advance(): jnp.einsum('gjrk,kgd->rgjd', probs.astype(jnp.bfloat16), value_rows, pref...  20 us
    all_to_all x1, blocking collectives, local(): lax.all_to_all(result, 'head', split_axis=2, concat_axis=3, tiled=True)  17 us
    dot_general x2, matrix products, advance(): jnp.einsum('rgjd,kgd->gjrk', query_rows, key_row_block, preferred_element...  14.3 us
    all_to_all x1, waiting for transfers between devices, local(): lax.all_to_all(query, 'head', split_axis=3, concat_axis=2, tiled=True)  14.1 us
    all_to_all x1, blocking collectives, local(): lax.all_to_all(stacked, 'head', split_axis=3, concat_axis=2, tiled=True)  10.1 us
    all_to_all x1, local copies, waits for them, and re-layouts, local(): lax.all_to_all(query, 'head', split_axis=3, concat_axis=2, tiled=True)  8.96 us
    reduce_sum x2, other arithmetic, advance(): totals = totals * rescale + jnp.sum(probs, axis=-1)  7.97 us
  transfers between devices with their start and end apart: 2, of which 2 were waited for; matrix products, arithmetic and copies ran while one was open for 19% of the time, Pallas kernels for 0%

commit v1 on v0

--- a/solution.py
+++ b/solution.py
@@ -7,6 +7,12 @@
 KEY_VALUE_HEADS = 8
 HEAD_WIDTH = 128
 BLK = 128
+
+
+def exchange_blocks(x, mesh_axis, split, join):
+    pieces = jnp.split(x, lax.axis_size(mesh_axis), axis=split)
+    received = lax.all_to_all(jnp.stack(pieces), mesh_axis, 0, 0)
+    return jnp.concatenate(received, axis=join)
 
 
 def doc_index(positions, doc_ends):
@@ -85,7 +91,7 @@
     row_max, totals, acc_sum = running
     result = (acc_sum / jnp.moveaxis(totals, 2, 0)[..., None]).astype(jnp.bfloat16)
     result = result.reshape(1, 2, span_len, kv_local * heads_per_group * HEAD_WIDTH)
-    return lax.all_to_all(result, "head", split_axis=2, concat_axis=3, tiled=True)
+    return exchange_blocks(result, "head", 2, 3)
 
 
 def solution(mesh):

time: 156 us -> 163 us (1.045)
  local copies, waits for them, and re-layouts: 46 us -> 53.6 us
    unnamed x10 -> x14, local copies, waits for them, and re-layouts: 23.3 us -> 29.3 us
    split x0 -> x1, local copies, waits for them, and re-layouts: none -> 4.92 us  [exchange_blocks(): pieces = jnp.split(x, lax.axis_size(mesh_axis), axis=split)]
    reshape x2 -> x1, local copies, waits for them, and re-layouts: 3.35 us -> 0.29 us  [local(): result.reshape(1, 2, span_len, kv_local * heads_per_group * HEAD_WIDTH)]
  transfers between devices with their start and end apart: 2 -> 2, of which waited for: 2 -> 2; matrix products, arithmetic and copies ran while one was open for 19% -> 18% of each run, Pallas kernels for 0% -> 0%
where the time goes in v1:
time: 163 us; the launch traced here: 162 us
  local copies, waits for them, and re-layouts  53.6 us (33%)
  matrix products  34.3 us (21%)
  blocking collectives  27 us (17%)
  waiting for transfers between devices  17 us (10%)
  between operations  13.6 us (8%)
  other arithmetic  12.7 us (8%)
  starting transfers between devices  3.7 us (2%)
    unnamed x14, local copies, waits for them, and re-layouts  29.3 us
    dot_general x2, matrix products, advance(): jnp.einsum('gjrk,kgd->rgjd', probs.astype(jnp.bfloat16), value_rows, pref...  20 us
    all_to_all x1, blocking collectives, exchange_blocks(): received = lax.all_to_all(jnp.stack(pieces), mesh_axis, 0, 0)  17 us
    dot_general x2, matrix products, advance(): jnp.einsum('rgjd,kgd->gjrk', query_rows, key_row_block, preferred_element...  14.3 us
    all_to_all x1, waiting for transfers between devices, local(): lax.all_to_all(query, 'head', split_axis=3, concat_axis=2, tiled=True)  13.9 us
    all_to_all x1, blocking collectives, local(): lax.all_to_all(stacked, 'head', split_axis=3, concat_axis=2, tiled=True)  10.1 us
    all_to_all x1, local copies, waits for them, and re-layouts, local(): lax.all_to_all(query, 'head', split_axis=3, concat_axis=2, tiled=True)  8.96 us
    reduce_sum x2, other arithmetic, advance(): totals = totals * rescale + jnp.sum(probs, axis=-1)  7.97 us
  transfers between devices with their start and end apart: 2, of which 2 were waited for; matrix products, arithmetic and copies ran while one was open for 18% of the time, Pallas kernels for 0%

profile of v1, /device:TPU:0, one launch (start us, length us, event | category | flops | bytes accessed | tf_op | source)
XLA Modules:
  0.0 162.0 jit_solution(12756936302469013470)
XLA Ops:
  6.5 2.2 %copy.40 = bf16[1,2,2,32,1024]{3,2,1,4,0:T(2,128)(2,1)S(1)} copy(bf16[1,2,2,32,1024]{4,3,2,1,0:T(8,128)(2,1)} %param.6) | data formatting | bytes 524288 | tf_op args[1]
  8.8 1.0 reshape.209
  9.7 10.1 %all_to_all.35 = bf16[4,2,16384]{2,1,0:T(2,128)(2,1)S(1)} all-to-all(bf16[4,2,16384]{2,1,0:T(2,128)(2,1)S(1)} %reshape.209), channel_id=1, replica_groups=mesh['ctx'=8,'head'=4] {'head'}, dimensions={0} | all-to-all | bytes 524288 | tf_op jit(solution)/shard_map/all_to_all | solution.py:30
  20.3 0.7 copy.52
  21.0 0.7 copy.42
  21.8 9.2 %copy.43 = bf16[1,2,32,8192]{2,1,0,3:T(2,128)(2,1)} copy(bf16[1,2,32,8192]{3,2,1,0:T(8,128)(2,1)} %param.5) | data formatting | bytes 2097152 | tf_op args[0]
  30.9 6.4 %reshape.211 = bf16[4,2,65536]{2,1,0:T(2,128)(2,1)} reshape(bf16[8192,1,2,32]{3,2,1,0:T(2,128)(2,1)} %bitcast.87) | data formatting | bytes 2097152
  37.3 3.7 %all-to-all-start.1 = ((bf16[4,2,65536]{2,1,0:T(2,128)(2,1)}), bf16[4,2,65536]{2,1,0:T(2,128)(2,1)S(1)}, u32[]{:S(2)}, u32[]{:S(2)}) async-start(bf16[4,2,65536]{2,1,0:T(2,128)(2,1)} %reshape.211), calls=%async_computation.1 | async-start | bytes 2097152 | tf_op jit(solution)/shard_map/all_to_all | solution.py:29
  41.4 13.9 %all-to-all-done.1 = bf16[4,2,65536]{2,1,0:T(2,128)(2,1)S(1)} async-done(((bf16[4,2,65536]{2,1,0:T(2,128)(2,1)}), bf16[4,2,65536]{2,1,0:T(2,128)(2,1)S(1)}, u32[]{:S(2)}, u32[]{:S(2)}) %all-to-all-start.1) | async-done | bytes 1048608 | tf_op jit(solution)/shard_map/all_to_all | solution.py:29
  55.3 3.5 %reshape.212 = bf16[8192,1,2,32]{3,2,1,0:T(2,128)(2,1)} reshape(bf16[4,2,65536]{2,1,0:T(2,128)(2,1)S(1)} %all-to-all-done.1) | data formatting | bytes 2097152
  58.8 9.0 %copy.44 = bf16[1,2,32,4,2048]{4,2,3,1,0:T(8,128)(2,1)S(1)} copy(bf16[1,2,32,4,2048]{2,1,4,3,0:T(2,128)(2,1)} %bitcast.86) | data formatting | bytes 2097152 | tf_op jit(solution)/shard_map/all_to_all | solution.py:29
  68.3 3.1 %all-gather.2.cloned.1.call-done = bf16[8,2,2,128,256]{4,3,2,1,0:T(8,128)(2,1)} async-done(((bf16[1,2,2,128,256]{4,3,2,1,0:T(8,128)(2,1)}), bf16[8,2,2,128,256]{4,3,2,1,0:T(8,128)(2,1)}) %all-gather.2.cloned.1.call-update) | async-done | bytes 2097168 | tf_op jit(solution)/shard_map/all_gather | solution.py:49
  71.3 52.6 %while.16 = (s32[]{:T(128)}, f32[2,8,256]{2,1,0:T(8,128)S(1)}, f32[2,8,256]{2,1,0:T(8,128)S(1)}, f32[256,2,8,128]{0,3,2,1:T(8,128)}, s32[256]{0:T(256)S(1)}, /*i...) while((s32[]{:T(128)}, f32[2,8,256]{2,1,0:T(8,128)S(1)}, ...), condition=%wide.region_6.7_spmd.clone.clone, body=%wide.region_2.6_spmd.clone.clone.sunk | while | flops 2204406784 | bytes 131365624 | solution.py:90
  71.9 0.6 subtract_multiply_fusion.2
  73.2 1.3 copy_bitcast_fusion.2
  74.7 7.2 %fusion.34 = (f32[2,8,256]{2,1,0:T(8,128)S(1)}, f32[2,1024,256,8]{2,1,3,0:T(8,128)}) fusion(pred[256,1024]{0,1:T(8,128)(4,1)S(1)} %compare_and_fusion.2, bf16[256,2,8,128]{3,0,2,1:T(8,128)(2,1)S(1)} %get-tuple-element.313, bf16[1024,2,128,1]{2,1,0,3:T(2,128)(2,1)S(1)} %bitcast.85), kind=kOutput, calls=%fused_computation.3.clone.1 | convolution fusion | flops 1086320640 | bytes 18628608 | tf_op jit(solution)/shard_map/while/body/eval_jaxpr/rgjd,kgd->gjrk/dot_general | solution.py:70
  82.0 9.7 %bitcast_add_fusion.2 = f32[256,2,8,128]{0,3,2,1:T(8,128)} fusion(f32[256,2,8,128]{0,3,2,1:T(8,128)} %get-tuple-element.295, f32[2,1024,256,8]{2,1,3,0:T(8,128)} %get-tuple-element.277, f32[2,8,256]{2,1,0:T(8,128)S(1)} %get-tuple-element.305, pred[256,1024]{0,1:T(8,128)(4,1)S(1)} %compare_and_fusion.2, f32[256,2,8]{0,2,1:T(8,128)S(1)} %get-tuple-element.278, ...), kind=kOutput, calls=%fused_computation.8.clone.1 | convolution fusion | flops 1096286208 | bytes 21790720 | tf_op jit(solution)/shard_map/while/body/eval_jaxpr/gjrk,kgd->rgjd/dot_general | solution.py:80
  91.7 1.6 copy-done
  93.3 4.0 %fusion.36 = f32[2,8,256]{2,1,0:T(8,128)S(1)} fusion(f32[2,1024,256,8]{2,1,3,0:T(8,128)S(1)} %copy-done, f32[2,8,256]{2,1,0:T(8,128)S(1)} %get-tuple-element.305, pred[256,1024]{0,1:T(8,128)(4,1)S(1)} %compare_and_fusion.2), kind=kLoop, calls=%fused_computation.5.clone.1 | loop fusion | flops 20967424 | bytes 17072128 | tf_op jit(solution)/shard_map/while/body/eval_jaxpr/reduce_sum | solution.py:79
  99.2 1.3 copy_bitcast_fusion.2
  100.7 7.2 %fusion.34 = (f32[2,8,256]{2,1,0:T(8,128)S(1)}, f32[2,1024,256,8]{2,1,3,0:T(8,128)}) fusion(pred[256,1024]{0,1:T(8,128)(4,1)S(1)} %compare_and_fusion.2, bf16[256,2,8,128]{3,0,2,1:T(8,128)(2,1)S(1)} %get-tuple-element.313, bf16[1024,2,128,1]{2,1,0,3:T(2,128)(2,1)S(1)} %bitcast.85), kind=kOutput, calls=%fused_computation.3.clone.1 | convolution fusion | flops 1086320640 | bytes 18628608 | tf_op jit(solution)/shard_map/while/body/eval_jaxpr/rgjd,kgd->gjrk/dot_general | solution.py:70
  108.0 10.3 %bitcast_add_fusion.2 = f32[256,2,8,128]{0,3,2,1:T(8,128)} fusion(f32[256,2,8,128]{0,3,2,1:T(8,128)} %get-tuple-element.295, f32[2,1024,256,8]{2,1,3,0:T(8,128)} %get-tuple-element.277, f32[2,8,256]{2,1,0:T(8,128)S(1)} %get-tuple-element.305, pred[256,1024]{0,1:T(8,128)(4,1)S(1)} %compare_and_fusion.2, f32[256,2,8]{0,2,1:T(8,128)S(1)} %get-tuple-element.278, ...), kind=kOutput, calls=%fused_computation.8.clone.1 | convolution fusion | flops 1096286208 | bytes 21790720 | tf_op jit(solution)/shard_map/while/body/eval_jaxpr/gjrk,kgd->rgjd/dot_general | solution.py:80
  118.3 1.6 copy-done
  119.9 4.0 %fusion.36 = f32[2,8,256]{2,1,0:T(8,128)S(1)} fusion(f32[2,1024,256,8]{2,1,3,0:T(8,128)S(1)} %copy-done, f32[2,8,256]{2,1,0:T(8,128)S(1)} %get-tuple-element.305, pred[256,1024]{0,1:T(8,128)(4,1)S(1)} %compare_and_fusion.2), kind=kLoop, calls=%fused_computation.5.clone.1 | loop fusion | flops 20967424 | bytes 17072128 | tf_op jit(solution)/shard_map/while/body/eval_jaxpr/reduce_sum | solution.py:79
  124.0 1.8 %divide_convert_fusion = bf16[256,2,8,128]{0,3,2,1:T(8,128)(2,1)S(1)} fusion(f32[256,2,8,128]{0,3,2,1:T(8,128)} %get-tuple-element.66, f32[256,2,8]{0,2,1:T(8,128)S(1)} %bitcast.103), kind=kLoop, calls=%fused_computation.31 | loop fusion | flops 1048576 | bytes 3162112 | tf_op jit(solution)/shard_map/convert_element_type | solution.py:92
  126.1 4.9 %fusion.20 = (bf16[1,2,32,2048]{2,1,3,0:T(2,128)(2,1)}, bf16[1,2,32,2048]{2,1,3,0:T(2,128)(2,1)S(1)}, bf16[1,2,32,2048]{2,1,3,0:T(2,128)(2,1)}, bf16[1,2,32,2048]{2,1,3,0:T(2,128)(2,1)S(1)}) fusion(bf16[1,2,128,2048]{2,1,3,0:T(2,128)(2,1)S(1)} %reshape.207), kind=kLoop, calls=%fused_computation.40 | loop fusion | bytes 2097152 | tf_op jit(solution)/shard_map/split | solution.py:13
  131.0 2.3 %copy.60 = bf16[1,2,32,2048]{3,2,1,0:T(8,128)(2,1)S(1)} copy(bf16[1,2,32,2048]{2,1,3,0:T(2,128)(2,1)} %get-tuple-element.197) | data formatting | bytes 524288
  133.3 2.3 %copy.61 = bf16[1,2,32,2048]{3,2,1,0:T(8,128)(2,1)S(1)} copy(bf16[1,2,32,2048]{2,1,3,0:T(2,128)(2,1)} %get-tuple-element.199) | data formatting | bytes 524288
  135.7 0.7 copy.62
  136.4 0.7 copy.63
  137.2 17.0 %all_to_all.36 = bf16[4,1,2,32,2048]{4,3,2,1,0:T(8,128)(2,1)S(1)} all-to-all(bf16[4,1,2,32,2048]{4,3,2,1,0:T(8,128)(2,1)S(1)} %pad_maximum_fusion), channel_id=1, replica_groups=mesh['ctx'=8,'head'=4] {'head'}, dimensions={0} | all-to-all | bytes 2097152 | tf_op jit(solution)/shard_map/all_to_all | solution.py:14
  154.2 1.0 copy.64
  (45 shorter events, 5.4 us)
Async XLA Ops:
  6.5 34.5 %copy-start.1 = (s32[4]{0:T(128)S(1)}, s32[4]{0:T(128)}, u32[]{:S(2)}) copy-start(s32[4]{0:T(128)} %param.7) | copy-start | bytes 52
  6.5 64.8 %all-gather.2.cloned.1.call-start = ((), (), s32[]{:S(2)}) async-start(), calls=%async_computation.3 | async-start | bytes 2359296 | tf_op jit(solution)/shard_map/all_gather | solution.py:49
  37.3 17.9 %all-to-all-start.1 = ((bf16[4,2,65536]{2,1,0:T(2,128)(2,1)}), bf16[4,2,65536]{2,1,0:T(2,128)(2,1)S(1)}, u32[]{:S(2)}, u32[]{:S(2)}) async-start(bf16[4,2,65536]{2,1,0:T(2,128)(2,1)} %reshape.211), calls=%async_computation.1 | async-start | bytes 2097152 | tf_op jit(solution)/shard_map/all_to_all | solution.py:29
  82.0 11.3 %copy-start = (f32[2,1024,256,8]{2,1,3,0:T(8,128)S(1)}, f32[2,1024,256,8]{2,1,3,0:T(8,128)}, u32[]{:S(2)}) copy-start(f32[2,1024,256,8]{2,1,3,0:T(8,128)} %get-tuple-element.277) | copy-start | bytes 50331652 | tf_op jit(solution)/shard_map/while
  108.0 11.9 %copy-start = (f32[2,1024,256,8]{2,1,3,0:T(8,128)S(1)}, f32[2,1024,256,8]{2,1,3,0:T(8,128)}, u32[]{:S(2)}) copy-start(f32[2,1024,256,8]{2,1,3,0:T(8,128)} %get-tuple-element.277) | copy-start | bytes 50331652 | tf_op jit(solution)/shard_map/while
Sparse Core Ops, SparseCore 0:
  21.9 49.4 all-gather.1
